TPU v7x, 512 devices: a whole 4x4x16 slice. The times are simulated.
512 devices in a mesh: row: 32 (over y_lo, z), col: 16 (over y_hi, x, core).
Axes of the slice: x: 4, y: 4 (y_hi: 2, y_lo: 2; y = y_hi * 2 + y_lo), z: 16, core: 2. Of those that a mesh axis runs over, the one named last changes fastest.
Arguments:
- image: bfloat16 [32, 2048, 2048], P(None, 'row', 'col'), may hold values from -6 to 6
- weight: bfloat16 [3, 3, 32, 32], replicated, may hold values from -0.375 to 0.375
- bias: float32 [32], replicated, may hold values from -3 to 3
- cotangent: bfloat16 [32, 2048, 2048], P(None, 'row', 'col'), may hold values from -60 to 60
Outputs:
- activation: bfloat16 [32, 2048, 2048], P(None, 'row', 'col')
- grad_image: bfloat16 [32, 2048, 2048], P(None, 'row', 'col')
- grad_weight: float32 [3, 3, 32, 32], replicated
- grad_bias: float32 [32], replicated
All inputs are finite; a program needn't handle non-finite values.
Results may differ from a plain program's by a relative error of at most 0.0065.
Values may be sent and summed in bfloat16 or wider, within the bound.
A program may use at most 64 MiB of HBM per device.

v0:
```python
import math
import jax
import jax.numpy as jnp
from jax import lax
from jax.sharding import PartitionSpec as P

DILATION_PIXELS = 16


def from_behind(value, axis, steps):
    count = lax.axis_size(axis)
    initial, last = (max(0, -steps), min(count, count - steps))
    return lax.ppermute(value, axis, [(source, source + steps) for source in range(initial, last)])


def gelu_pair(preact):
    coef = 0.7978845608
    cube = preact * preact * preact
    tval = jnp.tanh(coef * (preact + 0.044715 * cube))
    value = 0.5 * preact * (1.0 + tval)
    slope_val = 0.5 * (1.0 + tval) + 0.5 * preact * (1.0 - tval * tval) * coef * (
        1.0 + 3.0 * 0.044715 * preact * preact
    )
    return (value, slope_val)


def extended(local_block):
    row_count = local_block.shape[1]
    column_count = local_block.shape[2]
    upper_neighbour = from_behind(local_block[:, row_count - DILATION_PIXELS :, :], "row", 1)
    lower_neighbour = from_behind(local_block[:, :DILATION_PIXELS, :], "row", -1)
    tall_block = jnp.concatenate([upper_neighbour, local_block, lower_neighbour], axis=1)
    left_margin = from_behind(tall_block[:, :, column_count - DILATION_PIXELS :], "col", 1)
    right_margin = from_behind(tall_block[:, :, :DILATION_PIXELS], "col", -1)
    return jnp.concatenate([left_margin, tall_block, right_margin], axis=2)


def tap_view(ext, row_offset, column_offset, row_count, column_count):
    start_row = DILATION_PIXELS + row_offset * DILATION_PIXELS
    start_column = DILATION_PIXELS + column_offset * DILATION_PIXELS
    return ext[:, start_row : start_row + row_count, start_column : start_column + column_count]


def row_stack(ext, row_offset, sign_flip, row_count, column_count):
    return jnp.concatenate(
        [
            tap_view(
                ext, sign_flip * row_offset, sign_flip * column_offset, row_count, column_count
            )
            for column_offset in (-1, 0, 1)
        ],
        axis=0,
    )


def shards(image, weight, bias, cotangent):
    row_count = image.shape[1]
    column_count = image.shape[2]
    channels = image.shape[0]
    height_all = row_count * lax.axis_size("row")
    width_all = column_count * lax.axis_size("col")
    scale = 1.0 / math.sqrt(height_all * width_all)
    image_ext = extended(image)
    preact = jnp.zeros(image.shape, jnp.float32) + bias[:, None, None]
    for row_offset in (-1, 0, 1):
        weight_row = jnp.transpose(weight[row_offset + 1], (1, 0, 2)).reshape(
            channels, 3 * channels
        )
        stacked = row_stack(image_ext, row_offset, 1, row_count, column_count)
        preact = preact + jnp.einsum(
            "ok,krq->orq", weight_row, stacked, preferred_element_type=jnp.float32
        )
    value, slope_val = gelu_pair(preact)
    activation = value.astype(jnp.bfloat16)
    preact_gradient = (cotangent.astype(jnp.float32) * slope_val).astype(jnp.bfloat16)
    taps = []
    for row_offset in (-1, 0, 1):
        stacked = row_stack(image_ext, row_offset, 1, row_count, column_count)
        joined = (
            jnp.einsum("orq,krq->ok", preact_gradient, stacked, preferred_element_type=jnp.float32)
            * scale
        )
        taps.append(jnp.transpose(joined.reshape(channels, 3, channels), (1, 0, 2)))
    local_weight = jnp.stack(taps)
    local_bias = jnp.sum(preact_gradient.astype(jnp.float32), axis=(1, 2)) * scale
    grad_weight, grad_bias = lax.psum((local_weight, local_bias), ("row", "col"))
    grad_ext = extended(preact_gradient)
    total = jnp.zeros(image.shape, jnp.float32)
    for row_offset in (-1, 0, 1):
        weight_row = weight[row_offset + 1].reshape(3 * channels, channels)
        stacked = row_stack(grad_ext, row_offset, -1, row_count, column_count)
        total = total + jnp.einsum(
            "kc,krq->crq", weight_row, stacked, preferred_element_type=jnp.float32
        )
    grad_image = total.astype(jnp.bfloat16)
    return (activation, grad_image, grad_weight, grad_bias)


def solution(mesh):
    return jax.shard_map(
        shards,
        mesh=mesh,
        in_specs=(P(None, "row", "col"), P(), P(), P(None, "row", "col")),
        out_specs=(P(None, "row", "col"), P(None, "row", "col"), P(), P()),
        check_vma=False,
    )
```

profile of v0, /device:TPU:1, one launch (start us, length us, event | category | flops | bytes accessed | tf_op | source)
XLA Modules:
  0.0 181.4 jit_solution(1297893469584585609)
XLA Ops:
  0.6 1.4 copy.42
  2.1 4.4 %collective-permute-start = (bf16[32,16,128]{2,0,1:T(8,128)(2,1)S(1)}, bf16[32,16,128]{2,0,1:T(8,128)(2,1)S(1)}, u32[]{:S(2)}, u32[]{:S(2)}) collective-permute-start(bf16[32,16,128]{2,0,1:T(8,128)(2,1)S(1)} %get-tuple-element.42), channel_id=1, source_target_pairs={{0,16},{16,32},{32,48},{48,64},{64,80},{80,96},{96,112},{112,128},... | collective-permute-start | bytes 393224 | tf_op jit(solution)/shard_map/ppermute | solution.py:13
  6.5 1.3 collective-permute-start.1
  7.8 0.6 collective-permute-done
  8.4 0.4 constant_dynamic-update-slice_fusion.1
  8.8 3.6 %collective-permute-done.1 = bf16[32,16,128]{2,0,1:T(8,128)(2,1)S(1)} collective-permute-done((bf16[32,16,128]{2,0,1:T(8,128)(2,1)S(1)}, bf16[32,16,128]{2,0,1:T(8,128)(2,1)S(1)}, u32[]{:S(2)}, u32[]{:S(2)}) %collective-permute-start.1) | collective-permute-done | bytes 131104 | tf_op jit(solution)/shard_map/ppermute | solution.py:13
  12.4 0.3 fusion.68
  12.7 0.8 copy.45
  13.5 0.8 copy.48
  14.4 6.6 %collective-permute-start.3 = (bf16[32,96,16]{1,2,0:T(8,128)(2,1)S(1)}, bf16[32,96,16]{1,2,0:T(8,128)(2,1)S(1)}, u32[]{:S(2)}, u32[]{:S(2)}) collective-permute-start(bf16[32,96,16]{1,2,0:T(8,128)(2,1)S(1)} %copy.48), channel_id=1, source_target_pairs={{1,0},{2,1},{3,2},{4,3},{5,4},{6,5},{7,6},{8,7},{9,8},{10,9},{11,1... | collective-permute-start | bytes 294920 | tf_op jit(solution)/shard_map/ppermute | solution.py:13
  21.0 1.9 %collective-permute-start.2 = (bf16[32,96,16]{1,2,0:T(8,128)(2,1)S(1)}, bf16[32,96,16]{1,2,0:T(8,128)(2,1)S(1)}, u32[]{:S(2)}, u32[]{:S(2)}) collective-permute-start(bf16[32,96,16]{1,2,0:T(8,128)(2,1)S(1)} %copy.45), channel_id=1, source_target_pairs={{0,1},{1,2},{2,3},{3,4},{4,5},{5,6},{6,7},{7,8},{8,9},{9,10},{10,1... | collective-permute-start | bytes 294920 | tf_op jit(solution)/shard_map/ppermute | solution.py:13
  22.9 1.4 fusion.71
  24.5 0.7 reshape.34
  25.3 1.1 copy.46
  26.4 1.1 copy.49
  27.5 1.1 fusion.54
  28.7 0.3 fusion.50
  29.1 0.6 fusion.10
  29.7 0.2 copy-done.5
  30.0 0.4 fusion.31
  30.3 0.7 copy-done.11
  31.0 2.1 %convert_reduce_fusion = (f32[32]{0:T(128)S(1)}, bf16[32,64,128]{2,0,1:T(8,128)(2,1)S(1)}, bf16[32,64,128]{2,0,1:T(8,128)(2,1)}) fusion(bf16[32,64,128]{2,1,0:T(8,128)(2,1)S(1)} %copy-done.11, f32[64,128,32]{1,2,0:T(8,128)S(1)} %fusion.31, bf16[32,96,1]{1,0,2:T(8,128)(2,1)S(1)} %reshape.35, bf16[96,64,128]{2,0,1:T(8,128)(2,1)S(1)} %fusion.10), kind=kOutput, calls=%fused_computation.64 | convolution fusion | flops 56885216 | bytes 4200576 | tf_op jit(solution)/shard_map/ok,krq->orq/dot_general | solution.py:70
  33.1 0.6 fusion.38
  33.7 0.6 fusion.39
  34.5 0.3 copy-done.2
  34.8 0.6 fusion.40
  35.6 1.3 collective-permute-start.5
  36.9 4.0 %collective-permute-start.4 = (bf16[32,16,128]{2,0,1:T(8,128)(2,1)S(1)}, bf16[32,16,128]{2,0,1:T(8,128)(2,1)S(1)}, u32[]{:S(2)}, u32[]{:S(2)}) collective-permute-start(bf16[32,16,128]{2,0,1:T(8,128)(2,1)S(1)} %get-tuple-element.40), channel_id=1, source_target_pairs={{0,16},{16,32},{32,48},{48,64},{64,80},{80,96},{96,112},{112,128},... | collective-permute-start | bytes 393224 | tf_op jit(solution)/shard_map/ppermute | solution.py:13
  41.0 1.1 collective-permute-done.5
  42.1 0.8 collective-permute-done.4
  43.0 0.3 fusion.67
  43.3 0.8 copy.56
  44.1 0.8 copy.58
  44.9 5.1 %collective-permute-start.7 = (bf16[32,96,16]{1,2,0:T(8,128)(2,1)S(1)}, bf16[32,96,16]{1,2,0:T(8,128)(2,1)S(1)}, u32[]{:S(2)}, u32[]{:S(2)}) collective-permute-start(bf16[32,96,16]{1,2,0:T(8,128)(2,1)S(1)} %copy.58), channel_id=1, source_target_pairs={{0,1},{1,2},{2,3},{3,4},{4,5},{5,6},{6,7},{7,8},{8,9},{9,10},{10,1... | collective-permute-start | bytes 294920 | tf_op jit(solution)/shard_map/ppermute | solution.py:13
  50.0 2.1 %collective-permute-start.6 = (bf16[32,96,16]{1,2,0:T(8,128)(2,1)S(1)}, bf16[32,96,16]{1,2,0:T(8,128)(2,1)S(1)}, u32[]{:S(2)}, u32[]{:S(2)}) collective-permute-start(bf16[32,96,16]{1,2,0:T(8,128)(2,1)S(1)} %copy.56), channel_id=1, source_target_pairs={{1,0},{2,1},{3,2},{4,3},{5,4},{6,5},{7,6},{8,7},{9,8},{10,9},{11,1... | collective-permute-start | bytes 294920 | tf_op jit(solution)/shard_map/ppermute | solution.py:13
  52.2 120.2 %all-reduce = (f32[3,3,32,32]{3,1,2,0:T(4,128)S(1)}, f32[32]{0:T(128)}) all-reduce(f32[3,3,32,32]{3,1,2,0:T(4,128)S(1)} %pad_maximum_fusion.11, f32[32]{0:T(128)S(1)} %broadcast_multiply_fusion), channel_id=1, replica_groups=mesh['row'=32,'col'=16] {'row','col'}, use_global_device_ids=true, to_apply=%region_0.0 | all-reduce | flops 9248 | bytes 73984 | tf_op jit(solution)/shard_map/psum | solution.py:86
  172.4 0.7 copy.65
  173.1 1.0 copy.63
  174.1 1.1 copy.57
  175.2 1.1 copy.59
  176.3 1.5 pad_maximum_fusion.7
  177.8 0.7 fusion.65
  178.5 0.4 fusion.16
  178.9 0.4 copy-done.8
  179.3 0.4 fusion.2
  179.7 0.4 copy-done.7
  180.0 0.4 fusion.35
  180.4 1.0 copy.64
  (40 shorter events, 0.9 us)
Async XLA Ops:
  0.6 7.8 %copy-start = (bf16[32,64,128]{2,1,0:T(8,128)(2,1)S(1)}, bf16[32,64,128]{2,1,0:T(8,128)(2,1)}, u32[]{:S(2)}) copy-start(bf16[32,64,128]{2,1,0:T(8,128)(2,1)} %param.4) | copy-start | bytes 1572868
  2.1 6.3 %collective-permute-start = (bf16[32,16,128]{2,0,1:T(8,128)(2,1)S(1)}, bf16[32,16,128]{2,0,1:T(8,128)(2,1)S(1)}, u32[]{:S(2)}, u32[]{:S(2)}) collective-permute-start(bf16[32,16,128]{2,0,1:T(8,128)(2,1)S(1)} %get-tuple-element.42), channel_id=1, source_target_pairs={{0,16},{16,32},{32,48},{48,64},{64,80},{80,96},{96,112},{112,128},... | collective-permute-start | bytes 393224 | tf_op jit(solution)/shard_map/ppermute | solution.py:13
  6.5 5.9 %collective-permute-start.1 = (bf16[32,16,128]{2,0,1:T(8,128)(2,1)S(1)}, bf16[32,16,128]{2,0,1:T(8,128)(2,1)S(1)}, u32[]{:S(2)}, u32[]{:S(2)}) collective-permute-start(bf16[32,16,128]{2,0,1:T(8,128)(2,1)S(1)} %get-tuple-element.41), channel_id=1, source_target_pairs={{16,0},{32,16},{48,32},{64,48},{80,64},{96,80},{112,96},{128,112},... | collective-permute-start | bytes 393224 | tf_op jit(solution)/shard_map/ppermute | solution.py:13
  8.4 4.3 %copy-start.4 = (bf16[32,16,128]{2,0,1:T(8,128)(2,1)}, bf16[32,16,128]{2,0,1:T(8,128)(2,1)S(1)}, u32[]{:S(2)}) copy-start(bf16[32,16,128]{2,0,1:T(8,128)(2,1)S(1)} %collective-permute-done) | copy-start | bytes 393220
  14.4 12.0 %collective-permute-start.3 = (bf16[32,96,16]{1,2,0:T(8,128)(2,1)S(1)}, bf16[32,96,16]{1,2,0:T(8,128)(2,1)S(1)}, u32[]{:S(2)}, u32[]{:S(2)}) collective-permute-start(bf16[32,96,16]{1,2,0:T(8,128)(2,1)S(1)} %copy.48), channel_id=1, source_target_pairs={{1,0},{2,1},{3,2},{4,3},{5,4},{6,5},{7,6},{8,7},{9,8},{10,9},{11,1... | collective-permute-start | bytes 294920 | tf_op jit(solution)/shard_map/ppermute | solution.py:13
  21.0 4.3 %collective-permute-start.2 = (bf16[32,96,16]{1,2,0:T(8,128)(2,1)S(1)}, bf16[32,96,16]{1,2,0:T(8,128)(2,1)S(1)}, u32[]{:S(2)}, u32[]{:S(2)}) collective-permute-start(bf16[32,96,16]{1,2,0:T(8,128)(2,1)S(1)} %copy.45), channel_id=1, source_target_pairs={{0,1},{1,2},{2,3},{3,4},{4,5},{5,6},{6,7},{7,8},{8,9},{9,10},{10,1... | collective-permute-start | bytes 294920 | tf_op jit(solution)/shard_map/ppermute | solution.py:13
  27.5 1.2 copy-start.10
  28.7 1.0 copy-start.1
  29.1 0.9 copy-start.5
  29.1 0.9 copy-start.12
  30.0 1.0 copy-start.11
  33.7 1.1 copy-start.2
  33.7 1.1 copy-start.6
  35.6 6.5 %collective-permute-start.5 = (bf16[32,16,128]{2,0,1:T(8,128)(2,1)S(1)}, bf16[32,16,128]{2,0,1:T(8,128)(2,1)S(1)}, u32[]{:S(2)}, u32[]{:S(2)}) collective-permute-start(bf16[32,16,128]{2,0,1:T(8,128)(2,1)S(1)} %get-tuple-element.39), channel_id=1, source_target_pairs={{16,0},{32,16},{48,32},{64,48},{80,64},{96,80},{112,96},{128,112},... | collective-permute-start | bytes 393224 | tf_op jit(solution)/shard_map/ppermute | solution.py:13
  36.9 5.9 %collective-permute-start.4 = (bf16[32,16,128]{2,0,1:T(8,128)(2,1)S(1)}, bf16[32,16,128]{2,0,1:T(8,128)(2,1)S(1)}, u32[]{:S(2)}, u32[]{:S(2)}) collective-permute-start(bf16[32,16,128]{2,0,1:T(8,128)(2,1)S(1)} %get-tuple-element.40), channel_id=1, source_target_pairs={{0,16},{16,32},{32,48},{48,64},{64,80},{80,96},{96,112},{112,128},... | collective-permute-start | bytes 393224 | tf_op jit(solution)/shard_map/ppermute | solution.py:13
  43.3 129.8 %copy-start.3 = (bf16[32,64,128]{2,0,1:T(8,128)(2,1)S(1)}, bf16[32,64,128]{2,0,1:T(8,128)(2,1)}, u32[]{:S(2)}) copy-start(bf16[32,64,128]{2,0,1:T(8,128)(2,1)} %get-tuple-element.30) | copy-start | bytes 1572868
  44.9 130.3 %collective-permute-start.7 = (bf16[32,96,16]{1,2,0:T(8,128)(2,1)S(1)}, bf16[32,96,16]{1,2,0:T(8,128)(2,1)S(1)}, u32[]{:S(2)}, u32[]{:S(2)}) collective-permute-start(bf16[32,96,16]{1,2,0:T(8,128)(2,1)S(1)} %copy.58), channel_id=1, source_target_pairs={{0,1},{1,2},{2,3},{3,4},{4,5},{5,6},{6,7},{7,8},{8,9},{9,10},{10,1... | collective-permute-start | bytes 294920 | tf_op jit(solution)/shard_map/ppermute | solution.py:13
  50.0 124.1 %collective-permute-start.6 = (bf16[32,96,16]{1,2,0:T(8,128)(2,1)S(1)}, bf16[32,96,16]{1,2,0:T(8,128)(2,1)S(1)}, u32[]{:S(2)}, u32[]{:S(2)}) collective-permute-start(bf16[32,96,16]{1,2,0:T(8,128)(2,1)S(1)} %copy.56), channel_id=1, source_target_pairs={{1,0},{2,1},{3,2},{4,3},{5,4},{6,5},{7,6},{8,7},{9,8},{10,9},{11,1... | collective-permute-start | bytes 294920 | tf_op jit(solution)/shard_map/ppermute | solution.py:13
  177.8 0.7 copy-start.9
  178.5 0.7 copy-start.8
  179.3 0.7 copy-start.7
where the time goes:
time: 182 us; the launch traced here: 181 us
  blocking collectives  120 us (66%)
  starting transfers between devices  26.7 us (15%)
  local copies, waits for them, and re-layouts  18.2 us (10%)
  waiting for transfers between devices  6.11 us (3%)
  matrix products  5.82 us (3%)
  other arithmetic  3.41 us (2%)
    psum x1, blocking collectives, shards(): lax.psum((local_weight, local_bias), ('row', 'col'))  120 us
    ppermute x8, starting transfers between devices, from_behind(): lax.ppermute(value, axis, [(source, source + steps) for source in range(i...  26.7 us
    unnamed x32, local copies, waits for them, and re-layouts  6.49 us
    ppermute x8, waiting for transfers between devices, from_behind(): lax.ppermute(value, axis, [(source, source + steps) for source in range(i...  6.11 us
    ppermute x4, local copies, waits for them, and re-layouts, from_behind(): lax.ppermute(value, axis, [(source, source + steps) for source in range(i...  4.41 us
  transfers between devices with their start and end apart: 8, of which 4 were waited for; matrix products, arithmetic and copies ran while one was open for 4% of the time, Pallas kernels for 0%

commit v1 on v0

--- a/solution.py
+++ b/solution.py
@@ -83,7 +83,7 @@
         taps.append(jnp.transpose(joined.reshape(channels, 3, channels), (1, 0, 2)))
     local_weight = jnp.stack(taps)
     local_bias = jnp.sum(preact_gradient.astype(jnp.float32), axis=(1, 2)) * scale
-    grad_weight, grad_bias = lax.psum((local_weight, local_bias), ("row", "col"))
+    grad_weight, grad_bias = lax.psum(lax.psum((local_weight, local_bias), "col"), "row")
     grad_ext = extended(preact_gradient)
     total = jnp.zeros(image.shape, jnp.float32)
     for row_offset in (-1, 0, 1):

time: 182 us -> 267 us (1.47)
  the two profiles are of different devices: /device:TPU:1 before, /device:TPU:24 now
where the time goes in v1:
time: 267 us
  blocking collectives  187 us (70%)
  starting transfers between devices  36.2 us (14%)
  local copies, waits for them, and re-layouts  18.2 us (7%)
  waiting for transfers between devices  15 us (6%)
  matrix products  5.81 us (2%)
  other arithmetic  3.41 us (1%)
    psum x1, blocking collectives, shards(): lax.psum(lax.psum((local_weight, local_bias), 'col'), 'row')  120 us
    psum x1, blocking collectives, shards(): lax.psum((local_weight, local_bias), 'col')  67.2 us
    ppermute x8, starting transfers between devices, from_behind(): lax.ppermute(value, axis, [(source, source + steps) for source in range(i...  36.2 us
    ppermute x8, waiting for transfers between devices, from_behind(): lax.ppermute(value, axis, [(source, source + steps) for source in range(i...  15 us
    unnamed x32, local copies, waits for them, and re-layouts  6.49 us
  transfers between devices with their start and end apart: 8, of which 5 were waited for; matrix products, arithmetic and copies ran while one was open for 2% of the time, Pallas kernels for 0%

profile of v1, /device:TPU:24, one launch (start us, length us, event | category | flops | bytes accessed | tf_op | source)
XLA Modules:
  0.0 266.7 jit_solution(816818120320261366)
XLA Ops:
  0.6 1.4 copy.42
  2.1 3.8 %collective-permute-start = (bf16[32,16,128]{2,0,1:T(8,128)(2,1)S(1)}, bf16[32,16,128]{2,0,1:T(8,128)(2,1)S(1)}, u32[]{:S(2)}, u32[]{:S(2)}) collective-permute-start(bf16[32,16,128]{2,0,1:T(8,128)(2,1)S(1)} %get-tuple-element.44), channel_id=1, source_target_pairs={{0,16},{16,32},{32,48},{48,64},{64,80},{80,96},{96,112},{112,128},... | collective-permute-start | bytes 393224 | tf_op jit(solution)/shard_map/ppermute | solution.py:13
  6.0 9.7 %collective-permute-start.1 = (bf16[32,16,128]{2,0,1:T(8,128)(2,1)S(1)}, bf16[32,16,128]{2,0,1:T(8,128)(2,1)S(1)}, u32[]{:S(2)}, u32[]{:S(2)}) collective-permute-start(bf16[32,16,128]{2,0,1:T(8,128)(2,1)S(1)} %get-tuple-element.43), channel_id=1, source_target_pairs={{16,0},{32,16},{48,32},{64,48},{80,64},{96,80},{112,96},{128,112},... | collective-permute-start | bytes 393224 | tf_op jit(solution)/shard_map/ppermute | solution.py:13
  15.6 1.6 collective-permute-done
  17.2 0.4 constant_dynamic-update-slice_fusion.1
  17.6 0.8 collective-permute-done.1
  18.4 0.3 fusion.68
  18.7 0.8 copy.45
  19.5 0.8 copy.48
  20.4 3.6 %collective-permute-start.3 = (bf16[32,96,16]{1,2,0:T(8,128)(2,1)S(1)}, bf16[32,96,16]{1,2,0:T(8,128)(2,1)S(1)}, u32[]{:S(2)}, u32[]{:S(2)}) collective-permute-start(bf16[32,96,16]{1,2,0:T(8,128)(2,1)S(1)} %copy.48), channel_id=1, source_target_pairs={{1,0},{2,1},{3,2},{4,3},{5,4},{6,5},{7,6},{8,7},{9,8},{10,9},{11,1... | collective-permute-start | bytes 294920 | tf_op jit(solution)/shard_map/ppermute | solution.py:13
  24.0 1.9 collective-permute-start.2
  25.9 1.4 fusion.71
  27.5 0.7 reshape.34
  28.3 5.6 %collective-permute-done.2 = bf16[32,96,16]{1,2,0:T(8,128)(2,1)S(1)} collective-permute-done((bf16[32,96,16]{1,2,0:T(8,128)(2,1)S(1)}, bf16[32,96,16]{1,2,0:T(8,128)(2,1)S(1)}, u32[]{:S(2)}, u32[]{:S(2)}) %collective-permute-start.2) | collective-permute-done | bytes 98336 | tf_op jit(solution)/shard_map/ppermute | solution.py:13
  33.9 1.1 copy.46
  35.0 1.1 copy.49
  36.1 1.1 fusion.54
  37.3 0.3 fusion.50
  37.7 0.6 fusion.10
  38.6 0.4 fusion.31
  38.9 0.7 copy-done.11
  39.6 2.1 convert_reduce_fusion
  41.7 0.6 fusion.38
  42.3 0.6 fusion.39
  43.4 0.6 fusion.40
  44.2 5.9 %collective-permute-start.5 = (bf16[32,16,128]{2,0,1:T(8,128)(2,1)S(1)}, bf16[32,16,128]{2,0,1:T(8,128)(2,1)S(1)}, u32[]{:S(2)}, u32[]{:S(2)}) collective-permute-start(bf16[32,16,128]{2,0,1:T(8,128)(2,1)S(1)} %get-tuple-element.41), channel_id=1, source_target_pairs={{16,0},{32,16},{48,32},{64,48},{80,64},{96,80},{112,96},{128,112},... | collective-permute-start | bytes 393224 | tf_op jit(solution)/shard_map/ppermute | solution.py:13
  50.1 1.9 collective-permute-start.4
  52.1 0.6 collective-permute-done.5
  52.6 6.5 %collective-permute-done.4 = bf16[32,16,128]{2,0,1:T(8,128)(2,1)S(1)} collective-permute-done((bf16[32,16,128]{2,0,1:T(8,128)(2,1)S(1)}, bf16[32,16,128]{2,0,1:T(8,128)(2,1)S(1)}, u32[]{:S(2)}, u32[]{:S(2)}) %collective-permute-start.4) | collective-permute-done | bytes 131104 | tf_op jit(solution)/shard_map/ppermute | solution.py:13
  59.2 0.3 fusion.67
  59.5 0.8 copy.56
  60.3 0.8 copy.58
  61.2 1.9 collective-permute-start.7
  63.1 7.4 %collective-permute-start.6 = (bf16[32,96,16]{1,2,0:T(8,128)(2,1)S(1)}, bf16[32,96,16]{1,2,0:T(8,128)(2,1)S(1)}, u32[]{:S(2)}, u32[]{:S(2)}) collective-permute-start(bf16[32,96,16]{1,2,0:T(8,128)(2,1)S(1)} %copy.56), channel_id=1, source_target_pairs={{1,0},{2,1},{3,2},{4,3},{5,4},{6,5},{7,6},{8,7},{9,8},{10,9},{11,1... | collective-permute-start | bytes 294920 | tf_op jit(solution)/shard_map/ppermute | solution.py:13
  70.6 67.2 %all-reduce.1 = (f32[3,3,32,32]{3,1,2,0:T(4,128)S(1)}, f32[32]{0:T(128)S(1)}) all-reduce(f32[3,3,32,32]{3,1,2,0:T(4,128)S(1)} %pad_maximum_fusion.11, f32[32]{0:T(128)S(1)} %broadcast_multiply_fusion), channel_id=1, replica_groups=mesh['row'=32,'col'=16] {'col'}, use_global_device_ids=true, to_apply=%region_0.0 | all-reduce | flops 9248 | bytes 73984 | tf_op jit(solution)/shard_map/psum | solution.py:86
  137.8 119.8 %all-reduce = (f32[3,3,32,32]{3,1,2,0:T(4,128)S(1)}, f32[32]{0:T(128)}) all-reduce(f32[3,3,32,32]{3,1,2,0:T(4,128)S(1)} %get-tuple-element.18, f32[32]{0:T(128)S(1)} %get-tuple-element.19), channel_id=1, replica_groups=mesh['row'=32,'col'=16] {'row'}, use_global_device_ids=true, to_apply=%region_1.0 | all-reduce | flops 9248 | bytes 73984 | tf_op jit(solution)/shard_map/psum | solution.py:86
  257.7 0.7 copy.65
  258.4 1.0 copy.63
  259.4 1.1 copy.57
  260.5 1.1 copy.59
  261.6 1.5 pad_maximum_fusion.7
  263.1 0.7 fusion.65
  263.8 0.4 fusion.16
  264.2 0.4 copy-done.8
  264.6 0.4 fusion.2
  264.9 0.4 copy-done.7
  265.3 0.4 fusion.35
  265.7 1.0 copy.64
  (41 shorter events, 1.4 us)
Async XLA Ops:
  0.6 16.6 %copy-start = (bf16[32,64,128]{2,1,0:T(8,128)(2,1)S(1)}, bf16[32,64,128]{2,1,0:T(8,128)(2,1)}, u32[]{:S(2)}) copy-start(bf16[32,64,128]{2,1,0:T(8,128)(2,1)} %param.4) | copy-start | bytes 1572868
  2.1 15.1 %collective-permute-start = (bf16[32,16,128]{2,0,1:T(8,128)(2,1)S(1)}, bf16[32,16,128]{2,0,1:T(8,128)(2,1)S(1)}, u32[]{:S(2)}, u32[]{:S(2)}) collective-permute-start(bf16[32,16,128]{2,0,1:T(8,128)(2,1)S(1)} %get-tuple-element.44), channel_id=1, source_target_pairs={{0,16},{16,32},{32,48},{48,64},{64,80},{80,96},{96,112},{112,128},... | collective-permute-start | bytes 393224 | tf_op jit(solution)/shard_map/ppermute | solution.py:13
  6.0 12.4 %collective-permute-start.1 = (bf16[32,16,128]{2,0,1:T(8,128)(2,1)S(1)}, bf16[32,16,128]{2,0,1:T(8,128)(2,1)S(1)}, u32[]{:S(2)}, u32[]{:S(2)}) collective-permute-start(bf16[32,16,128]{2,0,1:T(8,128)(2,1)S(1)} %get-tuple-element.43), channel_id=1, source_target_pairs={{16,0},{32,16},{48,32},{64,48},{80,64},{96,80},{112,96},{128,112},... | collective-permute-start | bytes 393224 | tf_op jit(solution)/shard_map/ppermute | solution.py:13
  17.2 1.5 copy-start.4
  20.4 14.6 %collective-permute-start.3 = (bf16[32,96,16]{1,2,0:T(8,128)(2,1)S(1)}, bf16[32,96,16]{1,2,0:T(8,128)(2,1)S(1)}, u32[]{:S(2)}, u32[]{:S(2)}) collective-permute-start(bf16[32,96,16]{1,2,0:T(8,128)(2,1)S(1)} %copy.48), channel_id=1, source_target_pairs={{1,0},{2,1},{3,2},{4,3},{5,4},{6,5},{7,6},{8,7},{9,8},{10,9},{11,1... | collective-permute-start | bytes 294920 | tf_op jit(solution)/shard_map/ppermute | solution.py:13
  24.0 9.9 %collective-permute-start.2 = (bf16[32,96,16]{1,2,0:T(8,128)(2,1)S(1)}, bf16[32,96,16]{1,2,0:T(8,128)(2,1)S(1)}, u32[]{:S(2)}, u32[]{:S(2)}) collective-permute-start(bf16[32,96,16]{1,2,0:T(8,128)(2,1)S(1)} %copy.45), channel_id=1, source_target_pairs={{0,1},{1,2},{2,3},{3,4},{4,5},{5,6},{6,7},{7,8},{8,9},{9,10},{10,1... | collective-permute-start | bytes 294920 | tf_op jit(solution)/shard_map/ppermute | solution.py:13
  36.1 1.2 copy-start.10
  37.3 1.0 copy-start.1
  37.6 0.9 copy-start.5
  37.7 0.9 copy-start.12
  38.6 1.0 copy-start.11
  42.3 1.1 copy-start.2
  42.3 1.1 copy-start.6
  44.2 8.4 %collective-permute-start.5 = (bf16[32,16,128]{2,0,1:T(8,128)(2,1)S(1)}, bf16[32,16,128]{2,0,1:T(8,128)(2,1)S(1)}, u32[]{:S(2)}, u32[]{:S(2)}) collective-permute-start(bf16[32,16,128]{2,0,1:T(8,128)(2,1)S(1)} %get-tuple-element.41), channel_id=1, source_target_pairs={{16,0},{32,16},{48,32},{64,48},{80,64},{96,80},{112,96},{128,112},... | collective-permute-start | bytes 393224 | tf_op jit(solution)/shard_map/ppermute | solution.py:13
  50.1 9.0 %collective-permute-start.4 = (bf16[32,16,128]{2,0,1:T(8,128)(2,1)S(1)}, bf16[32,16,128]{2,0,1:T(8,128)(2,1)S(1)}, u32[]{:S(2)}, u32[]{:S(2)}) collective-permute-start(bf16[32,16,128]{2,0,1:T(8,128)(2,1)S(1)} %get-tuple-element.42), channel_id=1, source_target_pairs={{0,16},{16,32},{32,48},{48,64},{64,80},{80,96},{96,112},{112,128},... | collective-permute-start | bytes 393224 | tf_op jit(solution)/shard_map/ppermute | solution.py:13
  59.5 198.8 %copy-start.3 = (bf16[32,64,128]{2,0,1:T(8,128)(2,1)S(1)}, bf16[32,64,128]{2,0,1:T(8,128)(2,1)}, u32[]{:S(2)}) copy-start(bf16[32,64,128]{2,0,1:T(8,128)(2,1)} %get-tuple-element.32) | copy-start | bytes 1572868
  61.2 199.3 %collective-permute-start.7 = (bf16[32,96,16]{1,2,0:T(8,128)(2,1)S(1)}, bf16[32,96,16]{1,2,0:T(8,128)(2,1)S(1)}, u32[]{:S(2)}, u32[]{:S(2)}) collective-permute-start(bf16[32,96,16]{1,2,0:T(8,128)(2,1)S(1)} %copy.58), channel_id=1, source_target_pairs={{0,1},{1,2},{2,3},{3,4},{4,5},{5,6},{6,7},{7,8},{8,9},{9,10},{10,1... | collective-permute-start | bytes 294920 | tf_op jit(solution)/shard_map/ppermute | solution.py:13
  63.1 196.3 %collective-permute-start.6 = (bf16[32,96,16]{1,2,0:T(8,128)(2,1)S(1)}, bf16[32,96,16]{1,2,0:T(8,128)(2,1)S(1)}, u32[]{:S(2)}, u32[]{:S(2)}) collective-permute-start(bf16[32,96,16]{1,2,0:T(8,128)(2,1)S(1)} %copy.56), channel_id=1, source_target_pairs={{1,0},{2,1},{3,2},{4,3},{5,4},{6,5},{7,6},{8,7},{9,8},{10,9},{11,1... | collective-permute-start | bytes 294920 | tf_op jit(solution)/shard_map/ppermute | solution.py:13
  263.1 0.7 copy-start.9
  263.8 0.7 copy-start.8
  264.6 0.7 copy-start.7
